TPU v7x, 32 devices: a whole 2x2x4 slice. The times are simulated.
32 devices in a mesh: section: 4 (over z), seq: 8 (over y, x, core).
Axes of the slice: x: 2, y: 2, z: 4, core: 2. Of those that a mesh axis runs over, the one named last changes fastest.
Arguments:
- query_projection: bfloat16 [4, 2048, 4096], P('section', 'seq'), may hold values from -6 to 6
- k_proj: bfloat16 [4, 2048, 512], P('section', 'seq'), may hold values from -6 to 6
- value_projection: bfloat16 [4, 2048, 512], P('section', 'seq'), may hold values from -6 to 6
- doc_lengths: int32 [4, 8], P('section'), may hold values from 1 to 512, 2048 in all within a row
Outputs:
- next_rows: bfloat16 [4, 2048, 4096], P('section', 'seq')
Inputs may be any that keep to these rules, and one draw needn't show every extreme that they name: `doc_lengths`: in each section the largest length is exactly 512.
All inputs are finite; a program needn't handle non-finite values.
Results may differ from a plain program's by a relative error of at most 0.0037.
Values may be sent and summed in bfloat16 or wider, within the bound.
A program may use at most 64 MiB of HBM per device.

v0:
```python
import functools
import math

import jax
import jax.numpy as jnp
from jax import lax
from jax.experimental import pallas as pl
from jax.experimental.pallas import tpu as pltpu
from jax.sharding import PartitionSpec as P

QUERY_HEADS = 32
KEY_VALUE_HEADS = 4
HEAD_SIZE = 128
GROUP = QUERY_HEADS // KEY_VALUE_HEADS
MESH = pl.DeviceIdType.MESH
FACTOR = math.log2(math.e) / math.sqrt(HEAD_SIZE)


def kernel(
    n_seq, n_sec, q_ref, k_ref, v_ref, doc_ref, out_ref,
    q_buf, k_buf, v_buf, bias, stage,
    q_sem, own_sem, halo_send, halo_recv, out_send, out_recv,
):
    rows = q_ref.shape[0]
    me = lax.axis_index("seq")
    sec = lax.axis_index("section")
    to_one = lax.rem(me + 1, n_seq)
    to_two = lax.rem(me + 2, n_seq)
    from_one = lax.rem(me + n_seq - 1, n_seq)
    from_two = lax.rem(me + n_seq - 2, n_seq)
    next_sec = lax.rem(sec + 1, n_sec)
    last_sec = lax.rem(sec + n_sec - 1, n_sec)

    barrier = pltpu.get_barrier_semaphore()
    for other in (from_one, from_two, to_one, to_two):
        pl.semaphore_signal(
            barrier, inc=1, device_id={"seq": other}, device_id_type=MESH
        )
    for other in (next_sec, last_sec):
        pl.semaphore_signal(
            barrier, inc=1, device_id={"section": other}, device_id_type=MESH
        )

    def columns(head, count=1):
        return pl.ds(pl.multiple_of(head * HEAD_SIZE, HEAD_SIZE), count * HEAD_SIZE)

    def own_copy(source, buf, group, which):
        return pltpu.make_async_copy(
            source.at[:, columns(group)],
            buf.at[group, pl.ds(2 * rows, rows)],
            own_sem.at[group, which],
        )

    def q_copy(group):
        return pltpu.make_async_copy(
            q_ref.at[:, columns(group * GROUP, GROUP)],
            q_buf.at[:, columns(group * GROUP, GROUP)],
            q_sem.at[group],
        )

    def halo(source, buf, group, which, far):
        return pltpu.make_async_remote_copy(
            src_ref=source.at[:, columns(group)],
            dst_ref=buf.at[group, pl.ds(0 if far else rows, rows)],
            send_sem=halo_send.at[group, which, far],
            recv_sem=halo_recv.at[group, which, far],
            device_id={"seq": to_two if far else to_one},
            device_id_type=MESH,
        )

    def out_copy(head):
        return pltpu.make_async_remote_copy(
            src_ref=stage.at[:, columns(head)],
            dst_ref=out_ref.at[:, columns(head)],
            send_sem=out_send.at[head],
            recv_sem=out_recv.at[head],
            device_id={"section": next_sec},
            device_id_type=MESH,
        )

    pairs = ((k_ref, k_buf), (v_ref, v_buf))
    for group in range(KEY_VALUE_HEADS):
        for which, (source, buf) in enumerate(pairs):
            own_copy(source, buf, group, which).start()
        q_copy(group).start()

    pl.semaphore_wait(barrier, 6)
    for group in range(KEY_VALUE_HEADS):
        for which, (source, buf) in enumerate(pairs):
            for far in (1, 0):
                halo(source, buf, group, which, far).start()

    base = me * rows
    position = base + lax.broadcasted_iota(jnp.int32, (rows, rows), 0)
    column = lax.broadcasted_iota(jnp.int32, (rows, rows), 1)
    start = jnp.zeros((rows, rows), jnp.int32)
    end = jnp.int32(0)
    for doc in range(doc_ref.shape[1]):
        end = end + doc_ref[0, doc]
        start = jnp.where(end <= position, jnp.maximum(start, end), start)
    for place in range(3):
        key = base + (place - 2) * rows + column
        allowed = (key >= start) & (key <= position)
        bias[:, place * rows:(place + 1) * rows] = jnp.where(allowed, 0.0, -jnp.inf)

    for group in range(KEY_VALUE_HEADS):
        q_copy(group).wait()
        for which, (source, buf) in enumerate(pairs):
            own_copy(source, buf, group, which).wait()
            for far in (1, 0):
                halo(source, buf, group, which, far).wait_recv()

        @pl.loop(0, GROUP)
        def _(index):
            head = group * GROUP + index
            query = q_buf[:, columns(head)]
            scores = lax.dot_general(
                query, k_buf[group], (((1,), (1,)), ((), ())),
                preferred_element_type=jnp.float32,
            ) + bias[...]
            most = jnp.max(scores, axis=1, keepdims=True)
            weights = jnp.exp2((scores - most) * FACTOR)
            total = jnp.sum(weights, axis=1, keepdims=True)
            mixed = jnp.dot(
                weights.astype(jnp.bfloat16), v_buf[group],
                preferred_element_type=jnp.float32,
            )
            stage[:, columns(head)] = (mixed / total).astype(jnp.bfloat16)
            out_copy(head).start()

    for group in range(KEY_VALUE_HEADS):
        for which, (source, buf) in enumerate(pairs):
            for far in (1, 0):
                halo(source, buf, group, which, far).wait_send()

    @pl.loop(0, QUERY_HEADS)
    def _(head):
        out_copy(head).wait()


def solution(mesh):
    n_seq, n_sec = mesh.shape["seq"], mesh.shape["section"]

    def local(query_projection, k_proj, value_projection, doc_lengths):
        rows, width = query_projection.shape[1:]
        any_spec = pl.BlockSpec(memory_space=pl.ANY)
        result = pl.pallas_call(
            functools.partial(kernel, n_seq, n_sec),
            out_shape=jax.ShapeDtypeStruct((rows, width), jnp.bfloat16),
            in_specs=[any_spec] * 3 + [pl.BlockSpec(memory_space=pltpu.SMEM)],
            out_specs=any_spec,
            scratch_shapes=[
                pltpu.VMEM((rows, width), jnp.bfloat16),
                pltpu.VMEM((KEY_VALUE_HEADS, 3 * rows, HEAD_SIZE), jnp.bfloat16),
                pltpu.VMEM((KEY_VALUE_HEADS, 3 * rows, HEAD_SIZE), jnp.bfloat16),
                pltpu.VMEM((rows, 3 * rows), jnp.float32),
                pltpu.VMEM((rows, width), jnp.bfloat16),
                pltpu.SemaphoreType.DMA((KEY_VALUE_HEADS,)),
                pltpu.SemaphoreType.DMA((KEY_VALUE_HEADS, 2)),
                pltpu.SemaphoreType.DMA((KEY_VALUE_HEADS, 2, 2)),
                pltpu.SemaphoreType.DMA((KEY_VALUE_HEADS, 2, 2)),
                pltpu.SemaphoreType.DMA((QUERY_HEADS,)),
                pltpu.SemaphoreType.DMA((QUERY_HEADS,)),
            ],
            compiler_params=pltpu.CompilerParams(
                collective_id=0, has_side_effects=True
            ),
        )(query_projection[0], k_proj[0], value_projection[0], doc_lengths)
        return result[None]

    in_specs = (
        P("section", "seq", None),
        P("section", "seq", None),
        P("section", "seq", None),
        P("section", None),
    )
    return jax.shard_map(
        local, mesh=mesh, in_specs=in_specs, out_specs=P("section", "seq", None),
        check_vma=False,
    )
```

profile of v0, /device:TPU:0, one launch (start us, length us, event | category | flops | bytes accessed | tf_op | source)
XLA Modules:
  0.0 64.2 jit_solution(1005653249149809733)
XLA Ops:
  0.0 61.0 %shard_map.46 = bf16[256,4096]{1,0:T(8,128)(2,1)} custom-call(bf16[256,4096]{1,0:T(8,128)(2,1)} %bitcast.5, bf16[256,512]{1,0:T(8,128)(2,1)} %bitcast.6, bf16[256,512]{1,0:T(8,128)(2,1)} %bitcast.7, s32[1,8]{1,0:T(1,128)} %doc_ref.1), custom_call_target="tpu_custom_call" | custom-call | tf_op jit(solution)/shard_map/pallas_call | solution.py:147
  61.1 3.1 %copy.6 = bf16[1,256,4096]{2,1,0:T(8,128)(2,1)} copy(bf16[1,256,4096]{2,1,0:T(8,128)(2,1)} %bitcast.4) | data formatting | bytes 4194304
where the time goes:
time: 64.3 us; the launch traced here: 64.2 us
  Pallas kernels  61 us (95%)
  local copies, waits for them, and re-layouts  3.13 us (5%)
    pallas_call x1, Pallas kernels, local(): pl.pallas_call(functools.partial(kernel, n_seq, n_sec), out_shape=jax.Sha...  61 us
    unnamed x1, local copies, waits for them, and re-layouts  3.13 us

commit v1 on v0

--- a/solution.py
+++ b/solution.py
@@ -12,14 +12,16 @@
 KEY_VALUE_HEADS = 4
 HEAD_SIZE = 128
 GROUP = QUERY_HEADS // KEY_VALUE_HEADS
+RAW = 4
 MESH = pl.DeviceIdType.MESH
 FACTOR = math.log2(math.e) / math.sqrt(HEAD_SIZE)
 
 
 def kernel(
     n_seq, n_sec, q_ref, k_ref, v_ref, doc_ref, out_ref,
-    q_buf, k_buf, v_buf, bias, stage,
+    q_buf, k_buf, v_buf, bias, stage, doc_own, doc_last, raw_q, raw_k, raw_v,
     q_sem, own_sem, halo_send, halo_recv, out_send, out_recv,
+    doc_sem, raw_send, raw_recv, relay_send, relay_recv,
 ):
     rows = q_ref.shape[0]
     me = lax.axis_index("seq")
@@ -78,30 +80,79 @@
             device_id_type=MESH,
         )
 
+    def raw_copy(source, buf, which):
+        return pltpu.make_async_remote_copy(
+            src_ref=source,
+            dst_ref=buf,
+            send_sem=raw_send.at[which],
+            recv_sem=raw_recv.at[which],
+            device_id={"section": next_sec},
+            device_id_type=MESH,
+        )
+
+    def relay(buf, which, far):
+        return pltpu.make_async_remote_copy(
+            src_ref=buf.at[pl.ds(2 * rows, rows)],
+            dst_ref=buf.at[pl.ds(0 if far else rows, rows)],
+            send_sem=relay_send.at[which, far],
+            recv_sem=relay_recv.at[which, far],
+            device_id={"seq": to_two if far else to_one},
+            device_id_type=MESH,
+        )
+
+    raw_columns = pl.ds(0, RAW * HEAD_SIZE)
+    raw_copies = (
+        raw_copy(k_ref.at[:, pl.ds(0, HEAD_SIZE)], raw_k.at[pl.ds(2 * rows, rows)], 0),
+        raw_copy(v_ref.at[:, pl.ds(0, HEAD_SIZE)], raw_v.at[pl.ds(2 * rows, rows)], 1),
+        raw_copy(q_ref.at[:, raw_columns], raw_q, 2),
+        raw_copy(doc_ref, doc_last, 3),
+    )
+    doc_copy = pltpu.make_async_copy(doc_ref, doc_own, doc_sem)
+
     pairs = ((k_ref, k_buf), (v_ref, v_buf))
+    doc_copy.start()
     for group in range(KEY_VALUE_HEADS):
         for which, (source, buf) in enumerate(pairs):
             own_copy(source, buf, group, which).start()
         q_copy(group).start()
 
     pl.semaphore_wait(barrier, 6)
+    for copy in raw_copies:
+        copy.start()
     for group in range(KEY_VALUE_HEADS):
         for which, (source, buf) in enumerate(pairs):
             for far in (1, 0):
                 halo(source, buf, group, which, far).start()
 
-    base = me * rows
-    position = base + lax.broadcasted_iota(jnp.int32, (rows, rows), 0)
-    column = lax.broadcasted_iota(jnp.int32, (rows, rows), 1)
-    start = jnp.zeros((rows, rows), jnp.int32)
-    end = jnp.int32(0)
-    for doc in range(doc_ref.shape[1]):
-        end = end + doc_ref[0, doc]
-        start = jnp.where(end <= position, jnp.maximum(start, end), start)
-    for place in range(3):
-        key = base + (place - 2) * rows + column
-        allowed = (key >= start) & (key <= position)
-        bias[:, place * rows:(place + 1) * rows] = jnp.where(allowed, 0.0, -jnp.inf)
+    def fill_bias(docs):
+        base = me * rows
+        position = base + lax.broadcasted_iota(jnp.int32, (rows, rows), 0)
+        column = lax.broadcasted_iota(jnp.int32, (rows, rows), 1)
+        start = jnp.zeros((rows, rows), jnp.int32)
+        end = jnp.zeros((1, 1), jnp.int32)
+        for doc in range(docs.shape[1]):
+            end = end + docs[0:1, doc:doc + 1]
+            start = jnp.where(end <= position, jnp.maximum(start, end), start)
+        for place in range(3):
+            key = base + (place - 2) * rows + column
+            allowed = (key >= start) & (key <= position)
+            bias[:, place * rows:(place + 1) * rows] = jnp.where(allowed, 0.0, -jnp.inf)
+
+    def attend(query, keys, values):
+        scores = lax.dot_general(
+            query, keys, (((1,), (1,)), ((), ())),
+            preferred_element_type=jnp.float32,
+        ) + bias[...]
+        most = jnp.max(scores, axis=1, keepdims=True)
+        weights = jnp.exp2((scores - most) * FACTOR)
+        total = jnp.sum(weights, axis=1, keepdims=True)
+        mixed = jnp.dot(
+            weights.astype(jnp.bfloat16), values, preferred_element_type=jnp.float32
+        )
+        return (mixed / total).astype(jnp.bfloat16)
+
+    doc_copy.wait()
+    fill_bias(doc_own)
 
     for group in range(KEY_VALUE_HEADS):
         q_copy(group).wait()
@@ -110,30 +161,42 @@
             for far in (1, 0):
                 halo(source, buf, group, which, far).wait_recv()
 
-        @pl.loop(0, GROUP)
-        def _(index):
-            head = group * GROUP + index
-            query = q_buf[:, columns(head)]
-            scores = lax.dot_general(
-                query, k_buf[group], (((1,), (1,)), ((), ())),
-                preferred_element_type=jnp.float32,
-            ) + bias[...]
-            most = jnp.max(scores, axis=1, keepdims=True)
-            weights = jnp.exp2((scores - most) * FACTOR)
-            total = jnp.sum(weights, axis=1, keepdims=True)
-            mixed = jnp.dot(
-                weights.astype(jnp.bfloat16), v_buf[group],
-                preferred_element_type=jnp.float32,
+        @pl.loop(group * GROUP if group else RAW, (group + 1) * GROUP)
+        def _(head):
+            stage[:, columns(head)] = attend(
+                q_buf[:, columns(head)], k_buf[group], v_buf[group]
             )
-            stage[:, columns(head)] = (mixed / total).astype(jnp.bfloat16)
             out_copy(head).start()
 
+        if group == 1:
+            for copy in raw_copies:
+                copy.wait_recv()
+            for which, buf in enumerate((raw_k, raw_v)):
+                for far in (1, 0):
+                    relay(buf, which, far).start()
+
+    fill_bias(doc_last)
+    for which, buf in enumerate((raw_k, raw_v)):
+        for far in (1, 0):
+            relay(buf, which, far).wait_recv()
+
+    @pl.loop(0, RAW)
+    def _(head):
+        out_ref[:, columns(head)] = attend(
+            raw_q[:, columns(head)], raw_k[...], raw_v[...]
+        )
+
+    for copy in raw_copies:
+        copy.wait_send()
+    for which, buf in enumerate((raw_k, raw_v)):
+        for far in (1, 0):
+            relay(buf, which, far).wait_send()
     for group in range(KEY_VALUE_HEADS):
         for which, (source, buf) in enumerate(pairs):
             for far in (1, 0):
                 halo(source, buf, group, which, far).wait_send()
 
-    @pl.loop(0, QUERY_HEADS)
+    @pl.loop(RAW, QUERY_HEADS)
     def _(head):
         out_copy(head).wait()
 
@@ -143,29 +206,41 @@
 
     def local(query_projection, k_proj, value_projection, doc_lengths):
         rows, width = query_projection.shape[1:]
-        any_spec = pl.BlockSpec(memory_space=pl.ANY)
+        hbm_spec = pl.BlockSpec(memory_space=pltpu.HBM)
+        arrays = (query_projection[0], k_proj[0], value_projection[0], doc_lengths)
+        operands = [pltpu.with_memory_space_constraint(x, pltpu.HBM) for x in arrays]
         result = pl.pallas_call(
             functools.partial(kernel, n_seq, n_sec),
             out_shape=jax.ShapeDtypeStruct((rows, width), jnp.bfloat16),
-            in_specs=[any_spec] * 3 + [pl.BlockSpec(memory_space=pltpu.SMEM)],
-            out_specs=any_spec,
+            in_specs=[hbm_spec] * 4,
+            out_specs=pl.BlockSpec(memory_space=pltpu.VMEM),
             scratch_shapes=[
                 pltpu.VMEM((rows, width), jnp.bfloat16),
                 pltpu.VMEM((KEY_VALUE_HEADS, 3 * rows, HEAD_SIZE), jnp.bfloat16),
                 pltpu.VMEM((KEY_VALUE_HEADS, 3 * rows, HEAD_SIZE), jnp.bfloat16),
                 pltpu.VMEM((rows, 3 * rows), jnp.float32),
                 pltpu.VMEM((rows, width), jnp.bfloat16),
+                pltpu.VMEM(doc_lengths.shape, jnp.int32),
+                pltpu.VMEM(doc_lengths.shape, jnp.int32),
+                pltpu.VMEM((rows, RAW * HEAD_SIZE), jnp.bfloat16),
+                pltpu.VMEM((3 * rows, HEAD_SIZE), jnp.bfloat16),
+                pltpu.VMEM((3 * rows, HEAD_SIZE), jnp.bfloat16),
                 pltpu.SemaphoreType.DMA((KEY_VALUE_HEADS,)),
                 pltpu.SemaphoreType.DMA((KEY_VALUE_HEADS, 2)),
                 pltpu.SemaphoreType.DMA((KEY_VALUE_HEADS, 2, 2)),
                 pltpu.SemaphoreType.DMA((KEY_VALUE_HEADS, 2, 2)),
                 pltpu.SemaphoreType.DMA((QUERY_HEADS,)),
                 pltpu.SemaphoreType.DMA((QUERY_HEADS,)),
+                pltpu.SemaphoreType.DMA,
+                pltpu.SemaphoreType.DMA((4,)),
+                pltpu.SemaphoreType.DMA((4,)),
+                pltpu.SemaphoreType.DMA((2, 2)),
+                pltpu.SemaphoreType.DMA((2, 2)),
             ],
             compiler_params=pltpu.CompilerParams(
-                collective_id=0, has_side_effects=True
+                collective_id=0, has_side_effects=True, vmem_limit_bytes=24 * 2**20
             ),
-        )(query_projection[0], k_proj[0], value_projection[0], doc_lengths)
+        )(*operands)
         return result[None]
 
     in_specs = (

time: 64.3 us -> 58.5 us (0.910)
  Pallas kernels: 61 us -> 57 us
  local copies, waits for them, and re-layouts: 3.13 us -> 1.32 us
    pallas_call x1, Pallas kernels: 61 us -> 57 us  [local(): pl.pallas_call(functools.partial(kernel, n_seq, n_sec), out_shape=jax.Sha...]
    unnamed x1, local copies, waits for them, and re-layouts: 3.13 us -> 1.32 us
where the time goes in v1:
time: 58.5 us; the launch traced here: 58.4 us
  Pallas kernels  57 us (97%)
  local copies, waits for them, and re-layouts  1.32 us (2%)
    pallas_call x1, Pallas kernels, local(): pl.pallas_call(functools.partial(kernel, n_seq, n_sec), out_shape=jax.Sha...  57 us
    unnamed x1, local copies, waits for them, and re-layouts  1.32 us

profile of v1, /device:TPU:0, one launch (start us, length us, event | category | flops | bytes accessed | tf_op | source)
XLA Modules:
  0.0 58.4 jit_solution(14312950366292288819)
XLA Ops:
  0.0 57.0 %shard_map.46 = bf16[256,4096]{1,0:T(8,128)(2,1)S(1)} custom-call(bf16[256,4096]{1,0:T(8,128)(2,1)} %bitcast.5, bf16[256,512]{1,0:T(8,128)(2,1)} %bitcast.6, bf16[256,512]{1,0:T(8,128)(2,1)} %bitcast.7, s32[1,8]{1,0:T(1,128)} %doc_ref.1), custom_call_target="tpu_custom_call" | custom-call | tf_op jit(solution)/shard_map/pallas_call | solution.py:212
  57.0 1.3 %copy.6 = bf16[1,256,4096]{2,1,0:T(8,128)(2,1)} copy(bf16[1,256,4096]{2,1,0:T(8,128)(2,1)S(1)} %bitcast.4) | data formatting | bytes 4194304

commit v2 on v1

--- a/solution.py
+++ b/solution.py
@@ -12,7 +12,7 @@
 KEY_VALUE_HEADS = 4
 HEAD_SIZE = 128
 GROUP = QUERY_HEADS // KEY_VALUE_HEADS
-RAW = 4
+RAW = 5
 MESH = pl.DeviceIdType.MESH
 FACTOR = math.log2(math.e) / math.sqrt(HEAD_SIZE)
 
@@ -166,7 +166,10 @@
             stage[:, columns(head)] = attend(
                 q_buf[:, columns(head)], k_buf[group], v_buf[group]
             )
-            out_copy(head).start()
+
+            @pl.when(head > RAW)
+            def _():
+                out_copy(head - 1).start()
 
         if group == 1:
             for copy in raw_copies:
@@ -176,6 +179,7 @@
                     relay(buf, which, far).start()
 
     fill_bias(doc_last)
+    out_copy(QUERY_HEADS - 1).start()
     for which, buf in enumerate((raw_k, raw_v)):
         for far in (1, 0):
             relay(buf, which, far).wait_recv()

time: 58.5 us -> 58.5 us (level)
  no operation moved by 1% of the time
where the time goes in v2:
time: 58.5 us; the launch traced here: 58.4 us
  Pallas kernels  57 us (97%)
  local copies, waits for them, and re-layouts  1.32 us (2%)
    pallas_call x1, Pallas kernels, local(): pl.pallas_call(functools.partial(kernel, n_seq, n_sec), out_shape=jax.Sha...  57 us
    unnamed x1, local copies, waits for them, and re-layouts  1.32 us

profile of v2, /device:TPU:0, one launch (start us, length us, event | category | flops | bytes accessed | tf_op | source)
XLA Modules:
  0.0 58.4 jit_solution(14469944571170955572)
XLA Ops:
  0.0 57.0 %shard_map.46 = bf16[256,4096]{1,0:T(8,128)(2,1)S(1)} custom-call(bf16[256,4096]{1,0:T(8,128)(2,1)} %bitcast.5, bf16[256,512]{1,0:T(8,128)(2,1)} %bitcast.6, bf16[256,512]{1,0:T(8,128)(2,1)} %bitcast.7, s32[1,8]{1,0:T(1,128)} %doc_ref.1), custom_call_target="tpu_custom_call" | custom-call | tf_op jit(solution)/shard_map/pallas_call | solution.py:216
  57.0 1.3 %copy.6 = bf16[1,256,4096]{2,1,0:T(8,128)(2,1)} copy(bf16[1,256,4096]{2,1,0:T(8,128)(2,1)S(1)} %bitcast.4) | data formatting | bytes 4194304

commit v3 on v1

--- a/solution.py
+++ b/solution.py
@@ -12,7 +12,8 @@
 KEY_VALUE_HEADS = 4
 HEAD_SIZE = 128
 GROUP = QUERY_HEADS // KEY_VALUE_HEADS
-RAW = 4
+RAW = 5
+RAW_ODD = 3
 MESH = pl.DeviceIdType.MESH
 FACTOR = math.log2(math.e) / math.sqrt(HEAD_SIZE)
 
@@ -100,13 +101,17 @@
             device_id_type=MESH,
         )
 
-    raw_columns = pl.ds(0, RAW * HEAD_SIZE)
+    raw_columns = pl.ds(0, RAW_ODD * HEAD_SIZE)
+    more_columns = pl.ds(RAW_ODD * HEAD_SIZE, (RAW - RAW_ODD) * HEAD_SIZE)
+    even = lax.rem(me, 2) == 0
+    first = RAW - (RAW - RAW_ODD) * lax.rem(me, 2)
     raw_copies = (
         raw_copy(k_ref.at[:, pl.ds(0, HEAD_SIZE)], raw_k.at[pl.ds(2 * rows, rows)], 0),
         raw_copy(v_ref.at[:, pl.ds(0, HEAD_SIZE)], raw_v.at[pl.ds(2 * rows, rows)], 1),
-        raw_copy(q_ref.at[:, raw_columns], raw_q, 2),
+        raw_copy(q_ref.at[:, raw_columns], raw_q.at[:, raw_columns], 2),
         raw_copy(doc_ref, doc_last, 3),
     )
+    more_copy = raw_copy(q_ref.at[:, more_columns], raw_q.at[:, more_columns], 4)
     doc_copy = pltpu.make_async_copy(doc_ref, doc_own, doc_sem)
 
     pairs = ((k_ref, k_buf), (v_ref, v_buf))
@@ -119,6 +124,11 @@
     pl.semaphore_wait(barrier, 6)
     for copy in raw_copies:
         copy.start()
+
+    @pl.when(even)
+    def _():
+        more_copy.start()
+
     for group in range(KEY_VALUE_HEADS):
         for which, (source, buf) in enumerate(pairs):
             for far in (1, 0):
@@ -161,7 +171,7 @@
             for far in (1, 0):
                 halo(source, buf, group, which, far).wait_recv()
 
-        @pl.loop(group * GROUP if group else RAW, (group + 1) * GROUP)
+        @pl.loop(group * GROUP if group else first, (group + 1) * GROUP)
         def _(head):
             stage[:, columns(head)] = attend(
                 q_buf[:, columns(head)], k_buf[group], v_buf[group]
@@ -171,6 +181,11 @@
         if group == 1:
             for copy in raw_copies:
                 copy.wait_recv()
+
+            @pl.when(even)
+            def _():
+                more_copy.wait_recv()
+
             for which, buf in enumerate((raw_k, raw_v)):
                 for far in (1, 0):
                     relay(buf, which, far).start()
@@ -180,7 +195,7 @@
         for far in (1, 0):
             relay(buf, which, far).wait_recv()
 
-    @pl.loop(0, RAW)
+    @pl.loop(0, first)
     def _(head):
         out_ref[:, columns(head)] = attend(
             raw_q[:, columns(head)], raw_k[...], raw_v[...]
@@ -188,6 +203,11 @@
 
     for copy in raw_copies:
         copy.wait_send()
+
+    @pl.when(even)
+    def _():
+        more_copy.wait_send()
+
     for which, buf in enumerate((raw_k, raw_v)):
         for far in (1, 0):
             relay(buf, which, far).wait_send()
@@ -196,7 +216,7 @@
             for far in (1, 0):
                 halo(source, buf, group, which, far).wait_send()
 
-    @pl.loop(RAW, QUERY_HEADS)
+    @pl.loop(first, QUERY_HEADS)
     def _(head):
         out_copy(head).wait()
 
@@ -232,8 +252,8 @@
                 pltpu.SemaphoreType.DMA((QUERY_HEADS,)),
                 pltpu.SemaphoreType.DMA((QUERY_HEADS,)),
                 pltpu.SemaphoreType.DMA,
-                pltpu.SemaphoreType.DMA((4,)),
-                pltpu.SemaphoreType.DMA((4,)),
+                pltpu.SemaphoreType.DMA((5,)),
+                pltpu.SemaphoreType.DMA((5,)),
                 pltpu.SemaphoreType.DMA((2, 2)),
                 pltpu.SemaphoreType.DMA((2, 2)),
             ],

time: 58.5 us -> 58.5 us (level)
  no operation moved by 1% of the time
where the time goes in v3:
time: 58.5 us; the launch traced here: 58.4 us
  Pallas kernels  57 us (97%)
  local copies, waits for them, and re-layouts  1.32 us (2%)
    pallas_call x1, Pallas kernels, local(): pl.pallas_call(functools.partial(kernel, n_seq, n_sec), out_shape=jax.Sha...  57 us
    unnamed x1, local copies, waits for them, and re-layouts  1.32 us

profile of v3, /device:TPU:0, one launch (start us, length us, event | category | flops | bytes accessed | tf_op | source)
XLA Modules:
  0.0 58.4 jit_solution(5993560890028653665)
XLA Ops:
  0.0 57.0 %shard_map.46 = bf16[256,4096]{1,0:T(8,128)(2,1)S(1)} custom-call(bf16[256,4096]{1,0:T(8,128)(2,1)} %bitcast.5, bf16[256,512]{1,0:T(8,128)(2,1)} %bitcast.6, bf16[256,512]{1,0:T(8,128)(2,1)} %bitcast.7, s32[1,8]{1,0:T(1,128)} %doc_ref.1), custom_call_target="tpu_custom_call" | custom-call | tf_op jit(solution)/shard_map/pallas_call | solution.py:232
  57.0 1.3 %copy.6 = bf16[1,256,4096]{2,1,0:T(8,128)(2,1)} copy(bf16[1,256,4096]{2,1,0:T(8,128)(2,1)S(1)} %bitcast.4) | data formatting | bytes 4194304
